TPU v7x, 32 devices: a whole 2x2x4 slice. The times are simulated.
32 devices in a mesh: tenant: 2 (over x), store: 16 (over z, y, core).
Axes of the slice: x: 2, y: 2, z: 4, core: 2. Of those that a mesh axis runs over, the one named last changes fastest.
Arguments:
- queries: bfloat16 [4096, 1024], P(('tenant', 'store')), parts along dimension 0, may hold values from -24 to 24
- own_kv: bfloat16 [4096, 256], P(('tenant', 'store')), parts along dimension 0, may hold values from -15 to 15
- store_kv: bfloat16 [1024, 256, 256], P(('tenant', 'store')), parts along dimension 0, may hold values from -15 to 15
- q_start: int32 [32], P(('tenant', 'store')), parts along dimension 0, may hold values from 12288 to 16255
- pop_ids: int32 [8], P('tenant'), parts along dimension 0, may hold values from 0 to 511
- pop_pos: int32 [32, 4], P(('tenant', 'store')), parts along dimension 0, may hold values from 0 to 12287
- rare_ids: int32 [32, 6], P(('tenant', 'store')), parts along dimension 0, may hold values from 0 to 511, as said below
- rare_count: int32 [32], P(('tenant', 'store')), parts along dimension 0, may hold values from 4 to 6, as said below
- rare_pos: int32 [32, 6], P(('tenant', 'store')), parts along dimension 0, may hold values from 0 to 12287
Outputs:
- attended: bfloat16 [4096, 1024], P(('tenant', 'store')), parts along dimension 0
There are 2 independent parts, one for each index of `tenant`. A program takes and returns all parts, laid end to end along the dimension named above; each array names one. Nothing has to cross between parts.
Inputs may be any that keep to these rules, and one draw needn't show every extreme that they name: `rare_ids`: the first rare_count entries of one device's list name blocks of different holders (id // 32); entries after them are ignored. `rare_count`: some device requests exactly 6 blocks and another exactly 4.
All inputs are finite; a program needn't handle non-finite values.
Results may differ from a plain program's by a relative error of at most 0.0085.
The roundings to bfloat16 on the way count: a program that leaves them out, or rounds other values in their place, can miss the bound.
Values may be sent and summed in bfloat16 or wider, within the bound.
A program may use at most 128 MiB of HBM per device.

v0:
```python
import jax
import jax.numpy as jnp
from jax import lax
from jax.sharding import PartitionSpec as P


def rotate(values, positions, head_size):
    half_size = head_size // 2
    freq_table = 500000.0 ** (-(2.0 * jnp.arange(half_size, dtype=jnp.float32)) / head_size)
    angles = positions.astype(jnp.float32)[:, None] * freq_table[None, :]
    cosine = jnp.cos(angles)[:, None, :]
    sine_part = jnp.sin(angles)[:, None, :]
    shaped = values.reshape(values.shape[0], -1, 2, half_size)
    first_half = shaped[:, :, 0, :]
    second_half = shaped[:, :, 1, :]
    turned = jnp.stack(
        [
            first_half * cosine - second_half * sine_part,
            second_half * cosine + first_half * sine_part,
        ],
        axis=2,
    )
    return turned.reshape(values.shape)


def block_stats(query_rows, key_rows, value_rows, allowed, scale_factor):
    scores = jnp.dot(query_rows, key_rows.T, preferred_element_type=jnp.float32) * scale_factor
    scores = jnp.where(allowed, scores, -jnp.inf)
    top_score = jnp.max(scores, axis=1)
    weights = jnp.exp(scores - top_score[:, None]).astype(jnp.bfloat16)
    weight_sum = jnp.sum(weights.astype(jnp.float32), axis=1)
    mixed_part = jnp.dot(weights, value_rows, preferred_element_type=jnp.float32)
    return (top_score, weight_sum, mixed_part)


def combine(running, top_score, weight_sum, mixed_part):
    old_top, old_sum, old_mixed = running
    peak = jnp.maximum(old_top, top_score)
    keep_factor = jnp.exp(old_top - peak)
    take_factor = jnp.exp(top_score - peak)
    return (
        peak,
        old_sum * keep_factor + weight_sum * take_factor,
        old_mixed * keep_factor[:, None] + mixed_part * take_factor[:, None],
    )


def span_fold(running, query_rows, span_kv, offset, head_size, scale_factor):
    span_len = span_kv.shape[0]
    span_keys = rotate(
        span_kv[:, :head_size].astype(jnp.float32),
        offset + jnp.arange(span_len, dtype=jnp.int32),
        head_size,
    ).astype(jnp.bfloat16)
    top_score, weight_sum, mixed_part = block_stats(
        query_rows, span_keys, span_kv[:, head_size:], True, scale_factor
    )
    return combine(running, top_score, weight_sum, mixed_part)


def body(queries, own_kv, store_kv, q_start, pop_ids, pop_pos, rare_ids, rare_count, rare_pos):
    own_index = lax.axis_index("store")
    store_count = lax.axis_size("store")
    token_count = queries.shape[0]
    head_size = own_kv.shape[1] // 2
    group_size = queries.shape[1] // head_size
    per_device = store_kv.shape[0]
    span_len = store_kv.shape[1]
    kv_width = store_kv.shape[2]
    request_most = rare_ids.shape[1]
    scale_factor = head_size ** (-0.5)
    positions = q_start[0] + jnp.arange(token_count, dtype=jnp.int32)
    query_rows = (
        rotate(queries.astype(jnp.float32), positions, head_size)
        .astype(jnp.bfloat16)
        .reshape(token_count * group_size, head_size)
    )
    own_keys = rotate(own_kv[:, :head_size].astype(jnp.float32), positions, head_size).astype(
        jnp.bfloat16
    )
    causal = (jnp.arange(token_count * group_size) // group_size)[:, None] >= jnp.arange(
        token_count
    )[None, :]
    running = block_stats(query_rows, own_keys, own_kv[:, head_size:], causal, scale_factor)
    rare_list = rare_ids[0]
    is_request = jnp.arange(request_most) < rare_count[0]
    holder_index = rare_list // per_device
    slot_index = rare_list % per_device
    match_table = (
        holder_index[:, None] == jnp.arange(store_count, dtype=jnp.int32)[None, :]
    ) & is_request[:, None]
    asked = jnp.sum(jnp.where(match_table, slot_index[:, None] + 1, 0), axis=0) - 1
    asked_pos = jnp.sum(jnp.where(match_table, rare_pos[0][:, None], 0), axis=0)
    packed = jnp.stack([asked, asked_pos], axis=1)
    incoming = lax.all_to_all(packed, "store", split_axis=0, concat_axis=0, tiled=True)
    wanted_slot = incoming[:, 0]
    reply = jnp.take(store_kv, jnp.clip(wanted_slot, 0, per_device - 1), axis=0)
    reply = jnp.where((wanted_slot >= 0)[:, None, None], reply, jnp.zeros_like(reply))
    received = lax.all_to_all(reply, "store", split_axis=0, concat_axis=0, tiled=True)
    picked = jnp.take(store_kv, pop_ids % per_device, axis=0)
    holds_it = (pop_ids // per_device == own_index)[:, None, None]
    summed = lax.psum(jnp.where(holds_it, picked.astype(jnp.float32), 0.0), "store")
    popular_kv = summed.astype(jnp.bfloat16)
    for pop_index in range(pop_ids.shape[0]):
        running = span_fold(
            running,
            query_rows,
            popular_kv[pop_index],
            pop_pos[0, pop_index],
            head_size,
            scale_factor,
        )
    rare_kv = jnp.take(received, holder_index, axis=0)
    pair_count = request_most // 2
    paired_kv = rare_kv.reshape(pair_count, 2, span_len, kv_width)
    paired_pos = rare_pos[0].reshape(pair_count, 2)
    paired_live = is_request.reshape(pair_count, 2)

    def rare_step(carry, inputs):
        pair_kv, pair_pos, pair_live = inputs
        key_pos = (pair_pos[:, None] + jnp.arange(span_len, dtype=jnp.int32)[None, :]).reshape(-1)
        flat_kv = pair_kv.reshape(2 * span_len, kv_width)
        pair_keys = (
            rotate(flat_kv[:, :head_size].astype(jnp.float32), key_pos, head_size)
            .astype(jnp.bfloat16)
            .reshape(2, span_len, head_size)
        )
        scores = (
            jnp.einsum("rd,ckd->crk", query_rows, pair_keys, preferred_element_type=jnp.float32)
            * scale_factor
        )
        top_score = jnp.max(scores, axis=2)
        weights = jnp.exp(scores - top_score[:, :, None]).astype(jnp.bfloat16)
        weight_sum = jnp.sum(weights.astype(jnp.float32), axis=2)
        mixed_part = jnp.einsum(
            "crk,ckd->crd", weights, pair_kv[:, :, head_size:], preferred_element_type=jnp.float32
        )
        top_score = jnp.where(pair_live[:, None], top_score, -jnp.inf)
        carry = combine(carry, top_score[0], weight_sum[0], mixed_part[0])
        carry = combine(carry, top_score[1], weight_sum[1], mixed_part[1])
        return (carry, None)

    running, unused_out = lax.scan(rare_step, running, (paired_kv, paired_pos, paired_live))
    final_top, final_sum, final_mixed = running
    attended = final_mixed / final_sum[:, None]
    return attended.reshape(token_count, group_size * head_size).astype(jnp.bfloat16)


def solution(mesh):
    in_specs = (
        P(("tenant", "store"), None),
        P(("tenant", "store"), None),
        P(("tenant", "store"), None, None),
        P(("tenant", "store")),
        P("tenant"),
        P(("tenant", "store"), None),
        P(("tenant", "store"), None),
        P(("tenant", "store")),
        P(("tenant", "store"), None),
    )
    out_specs = P(("tenant", "store"), None)
    return jax.shard_map(body, mesh=mesh, in_specs=in_specs, out_specs=out_specs, check_vma=False)
```

profile of v0, /device:TPU:13, one launch (start us, length us, event | category | flops | bytes accessed | tf_op | source)
XLA Modules:
  0.0 171.5 jit_solution(15668158300816286855)
XLA Ops:
  0.0 0.7 and_select_fusion.2
  1.3 0.7 select_reduce_fusion.1
  2.1 0.7 copy.49
  2.8 6.6 %all-to-all-start = ((s32[16,1,2]{2,1,0:T(1,128)}), s32[16,1,2]{2,1,0:T(1,128)S(1)}, u32[]{:S(2)}, u32[]{:S(2)}) async-start(s32[16,1,2]{2,1,0:T(1,128)} %copy.49), calls=%async_computation | async-start | bytes 16384 | tf_op jit(solution)/shard_map/all_to_all | solution.py:95
  9.3 0.7 fusion.83
  10.0 0.7 compare_and_fusion.1
  10.7 2.8 %gather_fusion = bf16[4,256,256]{2,1,0:T(8,128)(2,1)S(1)} fusion(bf16[32,256,256]{2,1,0:T(8,128)(2,1)} %param.13, s32[1024]{0:T(1024)S(1)} %pad_clamp_fusion.2), kind=kCustom, calls=%fused_computation | custom fusion | bytes 1048592 | tf_op jit(solution)/shard_map/jit(_take)/gather | solution.py:100
  13.7 55.2 %all-reduce.1 = bf16[4,256,256]{2,1,0:T(8,128)(2,1)S(1)} all-reduce(f32[4,256,256]{2,1,0:T(8,128)S(1)} %convert_select_fusion), channel_id=1, replica_groups=mesh['tenant'=2,'store'=16] {'store'}, use_global_device_ids=true, to_apply=%region_1.2 | all-reduce | flops 262144 | bytes 1572864 | tf_op jit(solution)/shard_map/psum | solution.py:102
  69.3 0.6 fusion.89
  70.0 0.6 add_convert_fusion.3
  71.5 0.2 multiply_cosine_fusion.6
  71.9 0.5 copy.43
  72.4 0.2 convert_element_type.218
  72.7 0.6 add_convert_fusion.2
  73.5 0.2 fusion.72
  73.8 1.2 add_convert_fusion
  75.0 0.8 fusion.60
  75.8 0.6 pad_maximum_fusion.1
  76.4 0.3 fusion.56
  76.8 0.6 pad_maximum_fusion.4
  77.4 0.3 fusion.94
  77.7 0.5 broadcast.810
  78.2 0.6 reduce.6
  78.8 0.6 reduce.7
  79.5 0.7 reshape_squeeze.3
  80.2 0.6 compare_bitcast_fusion
  80.8 2.9 %gather_fusion.1 = bf16[16,256,256]{2,1,0:T(8,128)(2,1)S(1)} fusion(bf16[32,256,256]{2,1,0:T(8,128)(2,1)} %param.13, s32[1024]{0:T(1024)S(1)} %pad_clamp_fusion.1), kind=kCustom, calls=%fused_computation.1 | custom fusion | bytes 4194368 | tf_op jit(solution)/shard_map/jit(_take)/gather | solution.py:97
  83.7 2.3 %select_select_fusion = bf16[16,256,256]{2,1,0:T(8,128)(2,1)} fusion(bf16[16,256,256]{2,1,0:T(8,128)(2,1)S(1)} %gather_fusion.1, pred[16]{0:T(512)(128)(4,1)} %get-tuple-element.114, pred[16]{0:T(512)(128)(4,1)} %get-tuple-element.113), kind=kLoop, calls=%fused_computation.44 | loop fusion | flops 2097152 | bytes 4194336 | tf_op jit(solution)/shard_map/jit(_where)/select_n | solution.py:98
  85.9 22.9 %all-to-all-start.1 = ((bf16[16,256,256]{2,1,0:T(8,128)(2,1)}), bf16[16,256,256]{2,1,0:T(8,128)(2,1)}, u32[]{:S(2)}, u32[]{:S(2)}) async-start(bf16[16,256,256]{2,1,0:T(8,128)(2,1)} %select_select_fusion), calls=%async_computation.1 | async-start | bytes 4194304 | tf_op jit(solution)/shard_map/all_to_all | solution.py:99
  109.0 0.3 fusion.93
  109.3 0.2 convert_reduce_fusion.4
  109.5 0.3 fusion.91
  109.8 0.2 convert_reduce_fusion.2
  110.1 0.3 fusion.90
  110.5 0.2 convert_reduce_fusion.1
  110.7 0.3 fusion.92
  111.3 0.3 convolution_multiply_fusion.4
  111.6 0.5 fusion.30
  112.1 0.5 fusion.28
  112.7 0.5 fusion.26
  113.2 0.4 fusion.24
  113.5 42.9 %all-to-all-done.1 = bf16[16,256,256]{2,1,0:T(8,128)(2,1)} async-done(((bf16[16,256,256]{2,1,0:T(8,128)(2,1)}), bf16[16,256,256]{2,1,0:T(8,128)(2,1)}, u32[]{:S(2)}, u32[]{:S(2)}) %all-to-all-start.1) | async-done | bytes 2097184 | tf_op jit(solution)/shard_map/all_to_all | solution.py:99
  156.4 2.2 %gather_fusion.2 = bf16[6,256,256]{2,1,0:T(8,128)(2,1)S(1)} fusion(bf16[16,256,256]{2,1,0:T(8,128)(2,1)} %all-to-all-done.1, s32[1024]{0:T(1024)S(1)} %pad_clamp_fusion), kind=kCustom, calls=%fused_computation.2 | custom fusion | bytes 1572888 | tf_op jit(solution)/shard_map/jit(_take)/gather | solution.py:113
  158.7 11.8 %while.14 = (s32[]{:T(128)}, f32[1024]{0:T(1024)S(1)}, f32[1024]{0:T(1024)S(1)}, f32[1024,128]{1,0:T(8,128)S(1)}, pred[3,2]{1,0:T(4,128)(4,1)S(1)}, /*index=5*/b...) while((s32[]{:T(128)}, f32[1024]{0:T(1024)S(1)}, ...), condition=%wide.region_16.17_spmd, body=%wide.region_13.16_spmd.sunk | while | flops 274902208 | bytes 13001355 | solution.py:143
  158.9 0.7 fusion.117
  159.7 0.6 fusion.118
  160.3 0.5 bitcast_reduce_fusion.2
  160.9 0.6 fusion.122
  161.5 0.4 convert_reduce_fusion.7
  162.0 0.6 fusion.123
  162.9 0.7 fusion.117
  163.6 0.6 fusion.118
  164.3 0.5 bitcast_reduce_fusion.2
  164.8 0.6 fusion.122
  165.4 0.4 convert_reduce_fusion.7
  165.9 0.6 fusion.123
  166.8 0.7 fusion.117
  167.5 0.6 fusion.118
  168.2 0.5 bitcast_reduce_fusion.2
  168.7 0.6 fusion.122
  169.3 0.4 convert_reduce_fusion.7
  169.9 0.6 fusion.123
  170.5 0.2 divide_convert_fusion
  170.7 0.8 convert_element_type.241
  (98 shorter events, 3.4 us)
Async XLA Ops:
  2.8 77.4 %all-to-all-start = ((s32[16,1,2]{2,1,0:T(1,128)}), s32[16,1,2]{2,1,0:T(1,128)S(1)}, u32[]{:S(2)}, u32[]{:S(2)}) async-start(s32[16,1,2]{2,1,0:T(1,128)} %copy.49), calls=%async_computation | async-start | bytes 16384 | tf_op jit(solution)/shard_map/all_to_all | solution.py:95
  13.7 55.7 %copy-start.4 = (s32[1,4]{1,0:T(1,128)S(1)}, s32[1,4]{1,0:T(1,128)}, u32[]{:S(2)}) copy-start(s32[1,4]{1,0:T(1,128)} %param.16) | copy-start | bytes 52
  13.7 57.6 %copy-start = (bf16[128,1024]{1,0:T(8,128)(2,1)S(1)}, bf16[128,1024]{1,0:T(8,128)(2,1)}, u32[]{:S(2)}) copy-start(bf16[128,1024]{1,0:T(8,128)(2,1)} %param.11) | copy-start | bytes 786436
  71.5 1.9 %slice-start = ((bf16[128,256]{1,0:T(8,128)(2,1)}), bf16[128,128]{1,0:T(8,128)(2,1)S(1)}, s32[]{:S(2)}) async-start(bf16[128,256]{1,0:T(8,128)(2,1)} %param.12), calls=%async_computation.2 | async-start | bytes 65536 | tf_op jit(solution)/shard_map/slice | solution.py:78
  71.9 6.4 %copy-start.6 = (s32[1,6]{1,0:T(1,128)S(1)}, s32[1,6]{1,0:T(1,128)}, u32[]{:S(2)}) copy-start(s32[1,6]{1,0:T(1,128)} %param.17) | copy-start | bytes 76
  71.9 6.9 %copy-start.5 = (s32[1,6]{1,0:T(1,128)S(1)}, s32[1,6]{1,0:T(1,128)}, u32[]{:S(2)}) copy-start(s32[1,6]{1,0:T(1,128)} %param.19) | copy-start | bytes 76
  85.9 23.0 %copy-start.1 = (bf16[256,1,2,64]{0,3,2,1:T(8,128)(2,1)S(1)}, bf16[256,1,2,64]{0,3,2,1:T(8,128)(2,1)}, u32[]{:S(2)}) copy-start(bf16[256,1,2,64]{0,3,2,1:T(8,128)(2,1)} %pad_maximum_fusion.1) | copy-start | bytes 196612
  85.9 70.4 %all-to-all-start.1 = ((bf16[16,256,256]{2,1,0:T(8,128)(2,1)}), bf16[16,256,256]{2,1,0:T(8,128)(2,1)}, u32[]{:S(2)}, u32[]{:S(2)}) async-start(bf16[16,256,256]{2,1,0:T(8,128)(2,1)} %select_select_fusion), calls=%async_computation.1 | async-start | bytes 4194304 | tf_op jit(solution)/shard_map/all_to_all | solution.py:99
  109.3 0.8 copy-start.2
  110.5 0.8 copy-start.3
where the time goes:
time: 172 us
  blocking collectives  55.2 us (32%)
  waiting for transfers between devices  42.9 us (25%)
  starting transfers between devices  29.4 us (17%)
  other arithmetic  19 us (11%)
  local copies, waits for them, and re-layouts  15.8 us (9%)
  matrix products  7.16 us (4%)
  between operations  1.76 us (1%)
    psum x1, blocking collectives, body(): lax.psum(jnp.where(holds_it, picked.astype(jnp.float32), 0.0), 'store')  55.2 us
    all_to_all x1, waiting for transfers between devices, body(): lax.all_to_all(reply, 'store', split_axis=0, concat_axis=0, tiled=True)  42.9 us
    all_to_all x1, starting transfers between devices, body(): lax.all_to_all(reply, 'store', split_axis=0, concat_axis=0, tiled=True)  22.9 us
    all_to_all x1, starting transfers between devices, body(): lax.all_to_all(packed, 'store', split_axis=0, concat_axis=0, tiled=True)  6.55 us
  transfers between devices with their start and end apart: 2, of which 1 were waited for; matrix products, arithmetic and copies ran while one was open for 11% of the time, Pallas kernels for 0%

commit v1 on v0

--- a/solution.py
+++ b/solution.py
@@ -99,7 +99,9 @@
     received = lax.all_to_all(reply, "store", split_axis=0, concat_axis=0, tiled=True)
     picked = jnp.take(store_kv, pop_ids % per_device, axis=0)
     holds_it = (pop_ids // per_device == own_index)[:, None, None]
-    summed = lax.psum(jnp.where(holds_it, picked.astype(jnp.float32), 0.0), "store")
+    block = jnp.where(holds_it, picked.astype(jnp.float32), 0.0)
+    parts = lax.all_gather(block, "store")
+    summed = jnp.sum(parts, axis=0)
     popular_kv = summed.astype(jnp.bfloat16)
     for pop_index in range(pop_ids.shape[0]):
         running = span_fold(

time: 172 us -> 209 us (1.22); the launches traced: 172 us -> 206 us
  waiting for transfers between devices: 42.9 us -> 130 us
  blocking collectives: 55.2 us -> 10.1 us
  starting transfers between devices: 29.4 us -> 6.09 us
  between operations: 1.76 us -> 15.1 us
  other arithmetic: 19 us -> 23.6 us
  local copies, waits for them, and re-layouts: 15.8 us -> 12.6 us
    psum x1 -> x0, blocking collectives: 55.2 us -> none  [body(): lax.psum(jnp.where(holds_it, picked.astype(jnp.float32), 0.0), 'store')]
    all_gather x0 -> x1, waiting for transfers between devices: none -> 54.8 us  [body(): parts = lax.all_gather(block, 'store')]
    all_to_all x1, waiting for transfers between devices: 42.9 us -> 74.7 us  [body(): lax.all_to_all(reply, 'store', split_axis=0, concat_axis=0, tiled=True)]
    all_to_all x1, starting transfers between devices: 22.9 us -> 6.09 us  [body(): lax.all_to_all(reply, 'store', split_axis=0, concat_axis=0, tiled=True)]
    all_to_all x0 -> x1, blocking collectives: none -> 10.1 us  [body(): lax.all_to_all(packed, 'store', split_axis=0, concat_axis=0, tiled=True)]
    reduce_sum x0 -> x1, other arithmetic: none -> 7 us  [body(): summed = jnp.sum(parts, axis=0)]
    all_to_all x1 -> x0, starting transfers between devices: 6.55 us -> none  [body(): lax.all_to_all(packed, 'store', split_axis=0, concat_axis=0, tiled=True)]
  transfers between devices with their start and end apart: 2 -> 2, of which waited for: 1 -> 2; matrix products, arithmetic and copies ran while one was open for 11% -> 7% of each run, Pallas kernels for 0% -> 0%
where the time goes in v1:
time: 209 us; the launch traced here: 206 us
  waiting for transfers between devices  130 us (62%)
  other arithmetic  23.6 us (11%)
  between operations  15.1 us (7%)
  local copies, waits for them, and re-layouts  12.6 us (6%)
  blocking collectives  10.1 us (5%)
  matrix products  8.15 us (4%)
  starting transfers between devices  6.09 us (3%)
    all_to_all x1, waiting for transfers between devices, body(): lax.all_to_all(reply, 'store', split_axis=0, concat_axis=0, tiled=True)  74.7 us
    all_gather x1, waiting for transfers between devices, body(): parts = lax.all_gather(block, 'store')  54.8 us
    all_to_all x1, blocking collectives, body(): lax.all_to_all(packed, 'store', split_axis=0, concat_axis=0, tiled=True)  10.1 us
    reduce_sum x1, other arithmetic, body(): summed = jnp.sum(parts, axis=0)  7 us
    all_to_all x1, starting transfers between devices, body(): lax.all_to_all(reply, 'store', split_axis=0, concat_axis=0, tiled=True)  6.09 us
  transfers between devices with their start and end apart: 2, of which 2 were waited for; matrix products, arithmetic and copies ran while one was open for 7% of the time, Pallas kernels for 0%

profile of v1, /device:TPU:13, one launch (start us, length us, event | category | flops | bytes accessed | tf_op | source)
XLA Modules:
  0.0 205.6 jit_solution(9913602095612979880)
XLA Ops:
  6.5 0.7 compare_and_fusion.1
  7.2 2.8 %gather_fusion = bf16[4,256,256]{2,1,0:T(8,128)(2,1)S(1)} fusion(bf16[32,256,256]{2,1,0:T(8,128)(2,1)} %param.13, s32[1024]{0:T(1024)S(1)} %pad_clamp_fusion.2), kind=kCustom, calls=%fused_computation | custom fusion | bytes 1048592 | tf_op jit(solution)/shard_map/jit(_take)/gather | solution.py:100
  10.0 1.2 convert_select_fusion
  12.1 10.1 %all_to_all.17 = s32[16,1,2]{2,1,0:T(1,128)S(1)} all-to-all(s32[16,1,2]{2,1,0:T(1,128)S(1)} %copy.39), channel_id=1, replica_groups=mesh['tenant'=2,'store'=16] {'store'}, dimensions={0} | all-to-all | bytes 256 | tf_op jit(solution)/shard_map/all_to_all | solution.py:95
  22.3 3.2 %gather_fusion.1 = bf16[16,256,256]{2,1,0:T(8,128)(2,1)S(1)} fusion(bf16[32,256,256]{2,1,0:T(8,128)(2,1)} %param.13, s32[1024]{0:T(1024)S(1)} %pad_clamp_fusion.1), kind=kCustom, calls=%fused_computation.1 | custom fusion | bytes 4194368 | tf_op jit(solution)/shard_map/jit(_take)/gather | solution.py:97
  25.5 1.7 select_select_fusion
  27.2 6.1 %all-to-all-start.1 = ((bf16[16,256,256]{2,1,0:T(8,128)(2,1)}), bf16[16,256,256]{2,1,0:T(8,128)(2,1)S(1)}, u32[]{:S(2)}, u32[]{:S(2)}) async-start(bf16[16,256,256]{2,1,0:T(8,128)(2,1)} %select_select_fusion), calls=%async_computation.1 | async-start | bytes 4194304 | tf_op jit(solution)/shard_map/all_to_all | solution.py:99
  33.3 0.5 broadcast.838
  33.7 0.6 reduce.6
  34.3 0.6 reduce.7
  35.5 0.2 copy.32
  35.8 0.2 multiply_cosine_fusion.6
  36.1 0.5 copy.33
  36.6 0.2 convert_element_type.225
  36.9 0.1 copy.44
  37.2 0.7 fusion.89
  37.9 0.6 add_convert_fusion.3
  38.5 0.5 add_convert_fusion.2
  39.1 1.3 add_convert_fusion
  40.4 0.2 fusion.72
  40.6 0.3 fusion.94
  41.0 74.7 %all-to-all-done.1 = bf16[16,256,256]{2,1,0:T(8,128)(2,1)S(1)} async-done(((bf16[16,256,256]{2,1,0:T(8,128)(2,1)}), bf16[16,256,256]{2,1,0:T(8,128)(2,1)S(1)}, u32[]{:S(2)}, u32[]{:S(2)}) %all-to-all-start.1) | async-done | bytes 2097184 | tf_op jit(solution)/shard_map/all_to_all | solution.py:99
  115.7 1.5 gather_fusion.2
  117.2 1.3 broadcast_select_fusion.1
  118.5 54.8 %all-gather.2.cloned.1.call-done = f32[16,4,256,256]{3,2,1,0:T(8,128)} async-done(((f32[1,4,256,256]{3,2,1,0:T(8,128)}), f32[16,4,256,256]{3,2,1,0:T(8,128)}) %all-gather.2.cloned.1.call-update) | async-done | bytes 16777232 | tf_op jit(solution)/shard_map/all_gather | solution.py:103
  173.3 7.0 %reduce_sum.81 = bf16[4,256,256]{2,1,0:T(8,128)(2,1)S(1)} reduce(f32[16,4,256,256]{3,2,1,0:T(8,128)} %all-gather.2.cloned.1.call-done, f32[]{:T(128)} %constant.147.clone.1), dimensions={0}, to_apply=%region_1.2 | reduce | flops 3932160 | bytes 17301508 | tf_op jit(solution)/shard_map/reduce_sum | solution.py:104
  180.7 0.8 fusion.60
  181.5 1.3 fusion.93
  182.9 0.3 fusion.91
  183.2 0.1 copy.36
  183.3 0.3 fusion.56
  183.7 0.3 fusion.92
  184.0 0.5 copy-done
  184.6 0.2 convert_reduce_fusion.4
  184.7 0.2 convert_reduce_fusion.2
  184.9 0.3 fusion.90
  185.3 0.2 convert_reduce_fusion.3
  185.5 0.2 convert_reduce_fusion.1
  185.8 0.3 convolution_multiply_fusion.4
  186.1 0.5 fusion.30
  186.6 0.5 fusion.28
  187.1 0.5 fusion.26
  187.6 0.4 fusion.24
  188.0 9.7 %while.14 = (s32[]{:T(128)}, f32[1024]{0:T(1024)S(1)}, f32[1024]{0:T(1024)S(1)}, f32[1024,128]{1,0:T(8,128)S(1)}, pred[3,2]{1,0:T(4,128)(4,1)S(1)}, /*index=5*/b...) while((s32[]{:T(128)}, f32[1024]{0:T(1024)S(1)}, ...), condition=%wide.region_16.17_spmd, body=%wide.region_13.16_spmd.sunk | while | flops 274902208 | bytes 13001355 | solution.py:145
  188.0 0.1 copy.54
  188.3 0.6 fusion.118
  188.9 0.5 bitcast_reduce_fusion.2
  189.4 0.6 fusion.122
  190.1 0.4 convert_reduce_fusion.7
  190.6 0.6 fusion.123
  191.3 0.1 copy.54
  191.5 0.6 fusion.118
  192.2 0.5 bitcast_reduce_fusion.2
  192.7 0.6 fusion.122
  193.3 0.4 convert_reduce_fusion.7
  193.8 0.6 fusion.123
  194.5 0.1 copy.54
  194.8 0.6 fusion.118
  195.4 0.5 bitcast_reduce_fusion.2
  195.9 0.6 fusion.122
  196.6 0.4 convert_reduce_fusion.7
  197.1 0.6 fusion.123
  197.7 0.2 divide_convert_fusion
  197.9 0.8 convert_element_type.248
  (98 shorter events, 2.4 us)
Async XLA Ops:
  6.5 5.3 %copy-start.5 = (s32[1,6]{1,0:T(1,128)S(1)}, s32[1,6]{1,0:T(1,128)}, u32[]{:S(2)}) copy-start(s32[1,6]{1,0:T(1,128)} %param.17) | copy-start | bytes 76
  6.5 5.4 %copy-start.4 = (s32[1,6]{1,0:T(1,128)S(1)}, s32[1,6]{1,0:T(1,128)}, u32[]{:S(2)}) copy-start(s32[1,6]{1,0:T(1,128)} %param.19) | copy-start | bytes 76
  6.5 166.8 %all-gather.2.cloned.1.call-start = ((), (), s32[]{:S(2)}) async-start(), calls=%async_computation.2 | async-start | bytes 17825792 | tf_op jit(solution)/shard_map/all_gather | solution.py:103
  27.2 8.4 %copy-start.1 = (bf16[128,1024]{1,0:T(8,128)(2,1)S(1)}, bf16[128,1024]{1,0:T(8,128)(2,1)}, u32[]{:S(2)}) copy-start(bf16[128,1024]{1,0:T(8,128)(2,1)} %param.11) | copy-start | bytes 786436
  27.2 88.5 %all-to-all-start.1 = ((bf16[16,256,256]{2,1,0:T(8,128)(2,1)}), bf16[16,256,256]{2,1,0:T(8,128)(2,1)S(1)}, u32[]{:S(2)}, u32[]{:S(2)}) async-start(bf16[16,256,256]{2,1,0:T(8,128)(2,1)} %select_select_fusion), calls=%async_computation.1 | async-start | bytes 4194304 | tf_op jit(solution)/shard_map/all_to_all | solution.py:99
  35.5 1.4 slice-start
  35.7 1.5 copy-start.3
  183.3 1.2 copy-start
  184.9 0.8 copy-start.2
Sparse Core Ops, SparseCore 0:
  11.3 161.9 all-gather.1
